TPU v7x, 128 devices: a whole 4x4x4 slice. The times are simulated.
128 devices in a mesh: geo: 8 (over x, core), dist: 16 (over z, y).
Axes of the slice: x: 4, y: 4, z: 4, core: 2. Of those that a mesh axis runs over, the one named last changes fastest.
Arguments:
- estimates: bfloat16 [6144, 7424], P(('geo', 'dist')), may hold values from -4 to 4
- factors: bfloat16 [6144, 7424], P(('geo', 'dist')), may hold values from -0.625 to 0.625
- variances: bfloat16 [6144, 116], P(('geo', 'dist')), may hold values from 0.019897461 to 0.5
- intersection_tracts: int32 [2048, 32], P('dist'), may hold values from 0 to 6143, as said below
- intersection_weights: int32 [2048, 32], P('dist'), may hold values from 1 to 256
Outputs:
- marginal: float32 [2048, 7424], P('dist')
- covariance: float32 [2048, 13456], P('dist')
Inputs may be any that keep to these rules, and one draw needn't show every extreme that they name: `intersection_tracts`: each district's intersections are 32 different tracts among 64 consecutive ones, counted cyclically over the region.
All inputs are finite; a program needn't handle non-finite values.
Results may differ from a plain program's by a relative error of at most 0.0003.
Values may be sent and summed in bfloat16 or wider, within the bound.
A program may use at most 128 MiB of HBM per device.

v0:
```python
import jax
import jax.numpy as jnp
from jax import lax
from jax.sharding import PartitionSpec as P


def assemble(est_sum, fac_sum, var_sum):
    count = est_sum.shape[0]
    ages = var_sum.shape[1]
    shaped = fac_sum.reshape(count, ages, fac_sum.shape[1] // ages)
    outer = jnp.einsum("dik,djk->dij", shaped, shaped, precision=lax.Precision.HIGHEST)
    outer = outer + var_sum[:, :, None] * jnp.eye(ages, dtype=jnp.float32)[None, :, :]
    return (est_sum, outer.reshape(count, ages * ages))


def shards(estimates, factors, variances, intersection_tracts, intersection_weights):
    geo_index = lax.axis_index("geo")
    block = estimates.shape[0] * lax.axis_size("dist")
    local_ids = intersection_tracts - geo_index * block
    positions = jnp.arange(block, dtype=jnp.int32)
    onehot = (local_ids[:, :, None] == positions[None, None, :]).astype(jnp.float32)
    share = intersection_weights.astype(jnp.float32) / 256.0
    weight_mat = jnp.sum(onehot * share[:, :, None], axis=1).astype(jnp.bfloat16)
    square_mat = jnp.sum(onehot * (share * share)[:, :, None], axis=1)
    est_new = jnp.dot(
        weight_mat,
        lax.all_gather(estimates, "dist", axis=0, tiled=True),
        preferred_element_type=jnp.float32,
    )
    fac_new = jnp.dot(
        weight_mat,
        lax.all_gather(factors, "dist", axis=0, tiled=True),
        preferred_element_type=jnp.float32,
    )
    var_new = jnp.dot(
        square_mat,
        lax.all_gather(variances, "dist", axis=0, tiled=True).astype(jnp.float32),
        precision=lax.Precision.HIGHEST,
    )
    est_sum, fac_sum, var_sum = lax.psum((est_new, fac_new, var_new), "geo")
    return assemble(est_sum, fac_sum, var_sum)


def solution(mesh):
    return jax.shard_map(
        shards,
        mesh=mesh,
        in_specs=(
            P(("geo", "dist"), None),
            P(("geo", "dist"), None),
            P(("geo", "dist"), None),
            P("dist", None),
            P("dist", None),
        ),
        out_specs=(P("dist", None), P("dist", None)),
        check_vma=False,
    )
```

profile of v0, /device:TPU:1, one launch (start us, length us, event | category | flops | bytes accessed | tf_op | source)
XLA Modules:
  0.0 340.1 jit_solution(11527298273313712709)
XLA Ops:
  7.2 0.0 all-gather.5.cloned.1.call-start
  7.2 0.7 all-gather.5.cloned.1.call-update
  7.9 0.0 all-gather.3.cloned.1.call-start
  7.9 0.7 all-gather.3.cloned.1.call-update
  8.6 0.0 all-reduce.3.cloned.1.call-start
  8.7 0.7 convert_multiply_fusion
  9.4 0.1 copy.24
  9.5 0.7 broadcast_subtract_fusion
  10.2 0.1 copy.20
  10.3 0.1 copy.21
  10.4 13.2 %select_reduce_fusion = (f32[128,768]{1,0:T(8,128)S(1)}, bf16[128,768]{1,0:T(8,128)(2,1)S(1)}) fusion(f32[128,32]{1,0:T(8,128)S(1)} %copy.24, s32[128,32]{1,0:T(8,128)S(1)} %copy.20, f32[128,32]{1,0:T(8,128)S(1)} %copy.21), kind=kLoop, calls=%fused_computation | loop fusion | flops 15532032 | bytes 638976 | tf_op jit(solution)/shard_map/reduce_sum | solution.py:24
  23.6 74.5 %all-gather.5.cloned.1.call-done = bf16[768,7424]{1,0:T(8,128)(2,1)} async-done(((bf16[48,7424]{1,0:T(8,128)(2,1)}), bf16[768,7424]{1,0:T(8,128)(2,1)}) %all-gather.5.cloned.1.call-update) | async-done | bytes 11403280 | tf_op jit(solution)/shard_map/all_gather | solution.py:32
  98.1 10.6 %fusion.7 = f32[128,7424]{0,1:T(8,128)} fusion(bf16[128,768]{1,0:T(8,128)(2,1)S(1)} %get-tuple-element.5, bf16[768,7424]{1,0:T(8,128)(2,1)} %all-gather.5.cloned.1.call-done), kind=kOutput, calls=%fused_computation.14 | convolution fusion | flops 1459617792 | bytes 15400960 | tf_op jit(solution)/shard_map/dot_general | solution.py:30
  108.7 5.4 %copy.23 = f32[128,116,64]{1,2,0:T(8,128)} copy(f32[128,116,64]{0,2,1:T(8,128)} %bitcast.9) | data formatting | bytes 7602176 | tf_op jit(solution)/shard_map/reshape | solution.py:10
  114.2 0.0 copy-start
  114.2 70.4 %all-gather.3.cloned.1.call-done = bf16[768,7424]{1,0:T(8,128)(2,1)} async-done(((bf16[48,7424]{1,0:T(8,128)(2,1)}), bf16[768,7424]{1,0:T(8,128)(2,1)}) %all-gather.3.cloned.1.call-update) | async-done | bytes 11403280 | tf_op jit(solution)/shard_map/all_gather | solution.py:27
  184.5 7.8 %fusion.8 = f32[128,7424]{1,0:T(8,128)} fusion(bf16[128,768]{1,0:T(8,128)(2,1)S(1)} %get-tuple-element.5, bf16[768,7424]{1,0:T(8,128)(2,1)} %all-gather.3.cloned.1.call-done), kind=kOutput, calls=%fused_computation.15 | convolution fusion | flops 1459617792 | bytes 15400960 | tf_op jit(solution)/shard_map/dot_general | solution.py:25
  192.3 0.0 all-reduce.3.cloned.1.call-update
  192.3 0.0 copy-done
  192.3 19.1 %all_gather.11 = bf16[768,116]{1,0:T(8,128)(2,1)S(1)} all-gather(bf16[48,116]{1,0:T(8,128)(2,1)S(1)} %copy-done), channel_id=1, replica_groups=mesh['geo'=8,'dist'=16] {'dist'}, dimensions={0}, use_global_device_ids=true | all-gather | bytes 189312 | tf_op jit(solution)/shard_map/all_gather | solution.py:37
  211.5 0.4 fusion.6
  211.9 27.8 %psum.23 = f32[128,116]{0,1:T(8,128)S(1)} all-reduce(f32[128,116]{0,1:T(8,128)S(1)} %fusion.6), channel_id=1, replica_groups=mesh['geo'=8,'dist'=16] {'geo'}, use_global_device_ids=true, to_apply=%region_4.0 | all-reduce | flops 14848 | bytes 118784 | tf_op jit(solution)/shard_map/psum | solution.py:40
  239.6 0.1 copy.25
  239.7 52.9 %all-reduce.3.cloned.1.call-done = (f32[128,7424]{1,0:T(8,128)}, f32[128,116,64]{1,2,0:T(8,128)}) async-done(((f32[128,7424]{1,0:T(8,128)}, f32[128,116,64]{1,2,0:T(8,128)}), (f32[128,7424]{1,0:T(8,128)}, f32[128,116,64]{1,2,0:T(8,128)})) %all-reduce.3.cloned.1.call-update) | async-done | bytes 7602192 | tf_op jit(solution)/shard_map/psum | solution.py:40
  292.6 20.0 %multiply_add_fusion = f32[128,116,116]{2,1,0:T(8,128)} fusion(f32[116,116]{1,0:T(8,128)S(1)} %fusion.4, f32[128,116]{1,0:T(8,128)S(1)} %copy.25, f32[128,116,64]{1,2,0:T(8,128)} %get-tuple-element.7), kind=kOutput, calls=%fused_computation.3 | convolution fusion | flops 1326223360 | bytes 10803776 | tf_op jit(solution)/shard_map/dik,djk->dij/dot_general | solution.py:11
  312.6 8.5 %reshape.24 = f32[128,13456]{1,0:T(8,128)} reshape(f32[128,116,116]{2,1,0:T(8,128)} %multiply_add_fusion) | data formatting | bytes 13778944 | tf_op jit(solution)/shard_map/reshape | solution.py:13
  321.2 8.2 %copy.28 = f32[128,13456]{0,1:T(8,128)} copy(f32[128,13456]{1,0:T(8,128)} %reshape.24) | data formatting | bytes 13778944 | tf_op jit(solution)/shard_map/reshape | solution.py:13
  329.4 4.2 %copy.31 = f32[128,7424]{1,0:T(8,128)} copy(f32[128,7424]{1,0:T(8,128)} %get-tuple-element.10) | data formatting | bytes 7602176
  (1 shorter events, 0.0 us)
Async XLA Ops:
  7.2 90.9 %all-gather.5.cloned.1.call-start = ((), (), s32[]{:S(2)}) async-start(), calls=%async_computation.1 | async-start | bytes 12115968 | tf_op jit(solution)/shard_map/all_gather | solution.py:32
  7.9 176.6 %all-gather.3.cloned.1.call-start = ((), (), s32[]{:S(2)}) async-start(), calls=%async_computation | async-start | bytes 12115968 | tf_op jit(solution)/shard_map/all_gather | solution.py:27
  8.6 284.0 %all-reduce.3.cloned.1.call-start = ((), (), s32[]{:S(2)}) async-start(), calls=%async_computation.2 | async-start | bytes 15990784 | tf_op jit(solution)/shard_map/psum | solution.py:40
  114.2 78.2 %copy-start = (bf16[48,116]{1,0:T(8,128)(2,1)S(1)}, bf16[48,116]{1,0:T(8,128)(2,1)}, u32[]{:S(2)}) copy-start(bf16[48,116]{1,0:T(8,128)(2,1)} %param.7) | copy-start | bytes 33412
Sparse Core Ops, SparseCore 0:
  10.1 87.8 all-gather.4
  100.2 84.2 all-gather.2
  192.5 100.1 all-reduce.2
where the time goes:
time: 341 us; the launch traced here: 340 us
  waiting for transfers between devices  199 us (58%)
  blocking collectives  46.9 us (14%)
  matrix products  38.8 us (11%)
  local copies, waits for them, and re-layouts  26.8 us (8%)
  other arithmetic  14.6 us (4%)
  between operations  13.8 us (4%)
    all_gather x1, waiting for transfers between devices, shards(): lax.all_gather(factors, 'dist', axis=0, tiled=True)  74.5 us
    all_gather x1, waiting for transfers between devices, shards(): lax.all_gather(estimates, 'dist', axis=0, tiled=True)  70.4 us
    psum x1, waiting for transfers between devices, shards(): est_sum, fac_sum, var_sum = lax.psum((est_new, fac_new, var_new), 'geo')  52.9 us
    psum x1, blocking collectives, shards(): est_sum, fac_sum, var_sum = lax.psum((est_new, fac_new, var_new), 'geo')  27.8 us
    dot_general x1, matrix products, assemble(): jnp.einsum('dik,djk->dij', shaped, shaped, precision=lax.Precision.HIGHEST)  20 us
    all_gather x1, blocking collectives, shards(): lax.all_gather(variances, 'dist', axis=0, tiled=True).astype(jnp.float32)  19.1 us
    reshape x2, local copies, waits for them, and re-layouts, assemble(): return (est_sum, outer.reshape(count, ages * ages))  16.8 us
    reduce_sum x1, other arithmetic, shards(): square_mat = jnp.sum(onehot * (share * share)[:, :, None], axis=1)  13.2 us
  transfers between devices with their start and end apart: 3, of which 3 were waited for; matrix products, arithmetic and copies ran while one was open for 9% of the time, Pallas kernels for 0%

commit v1 on v0

--- a/solution.py
+++ b/solution.py
@@ -2,6 +2,11 @@
 import jax.numpy as jnp
 from jax import lax
 from jax.sharding import PartitionSpec as P
+
+
+def swapped_in(value, name, dim):
+    outgoing = jnp.stack([value] * lax.axis_size(name))
+    return jnp.concatenate(lax.all_to_all(outgoing, name, 0, 0), axis=dim)
 
 
 def assemble(est_sum, fac_sum, var_sum):
@@ -28,9 +33,7 @@
         preferred_element_type=jnp.float32,
     )
     fac_new = jnp.dot(
-        weight_mat,
-        lax.all_gather(factors, "dist", axis=0, tiled=True),
-        preferred_element_type=jnp.float32,
+        weight_mat, swapped_in(factors, "dist", 0), preferred_element_type=jnp.float32
     )
     var_new = jnp.dot(
         square_mat,

time: 341 us -> 404 us (1.18)
  waiting for transfers between devices: 199 us -> 247 us
  starting transfers between devices: 0.11 us -> 8.85 us
  local copies, waits for them, and re-layouts: 26.8 us -> 32.6 us
    all_to_all x0 -> x1, waiting for transfers between devices: none -> 192 us  [swapped_in(): return jnp.concatenate(lax.all_to_all(outgoing, name, 0, 0), axis=dim)]
    all_gather x1 -> x0, waiting for transfers between devices: 74.5 us -> none  [shards(): lax.all_gather(factors, 'dist', axis=0, tiled=True)]
    all_gather x1, waiting for transfers between devices: 70.4 us -> 0.01 us  [shards(): lax.all_gather(estimates, 'dist', axis=0, tiled=True)]
    all_to_all x0 -> x1, starting transfers between devices: none -> 8.77 us  [swapped_in(): return jnp.concatenate(lax.all_to_all(outgoing, name, 0, 0), axis=dim)]
    another operation x0 -> x1, local copies, waits for them, and re-layouts: none -> 5.99 us  [swapped_in(): outgoing = jnp.stack([value] * lax.axis_size(name))]
  transfers between devices with their start and end apart: 3 -> 3, of which waited for: 3 -> 2; matrix products, arithmetic and copies ran while one was open for 9% -> 9% of each run, Pallas kernels for 0% -> 0%
where the time goes in v1:
time: 404 us
  waiting for transfers between devices  247 us (61%)
  blocking collectives  49.7 us (12%)
  matrix products  38.8 us (10%)
  local copies, waits for them, and re-layouts  32.6 us (8%)
  between operations  14.1 us (3%)
  other arithmetic  13.2 us (3%)
  starting transfers between devices  8.85 us (2%)
    all_to_all x1, waiting for transfers between devices, swapped_in(): return jnp.concatenate(lax.all_to_all(outgoing, name, 0, 0), axis=dim)  192 us
    psum x1, waiting for transfers between devices, shards(): est_sum, fac_sum, var_sum = lax.psum((est_new, fac_new, var_new), 'geo')  53.8 us
    psum x1, blocking collectives, shards(): est_sum, fac_sum, var_sum = lax.psum((est_new, fac_new, var_new), 'geo')  27.7 us
    all_gather x1, blocking collectives, shards(): lax.all_gather(variances, 'dist', axis=0, tiled=True).astype(jnp.float32)  22 us
    dot_general x1, matrix products, assemble(): jnp.einsum('dik,djk->dij', shaped, shaped, precision=lax.Precision.HIGHEST)  20 us
    reshape x2, local copies, waits for them, and re-layouts, assemble(): return (est_sum, outer.reshape(count, ages * ages))  16.7 us
    reduce_sum x1, other arithmetic, shards(): square_mat = jnp.sum(onehot * (share * share)[:, :, None], axis=1)  13.2 us
    dot_general x1, matrix products, shards(): jnp.dot(weight_mat, swapped_in(factors, 'dist', 0), preferred_element_typ...  10.6 us
  transfers between devices with their start and end apart: 3, of which 2 were waited for; matrix products, arithmetic and copies ran while one was open for 9% of the time, Pallas kernels for 0%

profile of v1, /device:TPU:1, one launch (start us, length us, event | category | flops | bytes accessed | tf_op | source)
XLA Modules:
  0.0 403.7 jit_solution(14390370973777757755)
XLA Ops:
  7.2 0.0 all-gather.2.cloned.1.call-start
  7.2 0.7 all-gather.2.cloned.1.call-update
  7.9 6.0 %stack.2 = bf16[16,48,7424]{2,1,0:T(8,128)(2,1)} broadcast(bf16[48,7424]{1,0:T(8,128)(2,1)} %param.6), dimensions={1,2} | broadcast | bytes 12115968 | tf_op jit(solution)/shard_map/stack | solution.py:8
  13.9 0.0 copy-start
  13.9 0.0 copy-start.1
  13.9 8.8 %all-to-all-start = ((bf16[16,48,7424]{2,1,0:T(8,128)(2,1)}), bf16[16,48,7424]{2,1,0:T(8,128)(2,1)}, u32[]{:S(2)}, u32[]{:S(2)}) async-start(bf16[16,48,7424]{2,1,0:T(8,128)(2,1)} %stack.2), calls=%async_computation | async-start | bytes 22806528 | tf_op jit(solution)/shard_map/all_to_all | solution.py:9
  22.7 0.0 all-reduce.3.cloned.1.call-start
  22.7 0.0 copy-done
  22.7 0.1 copy.21
  22.8 0.1 copy.24
  22.9 0.0 copy-done.1
  23.0 0.1 copy.20
  23.1 13.2 %select_reduce_fusion = (f32[128,768]{1,0:T(8,128)S(1)}, bf16[128,768]{1,0:T(8,128)(2,1)S(1)}) fusion(f32[128,32]{1,0:T(8,128)S(1)} %copy.24, s32[128,32]{1,0:T(8,128)S(1)} %copy.20, f32[128,32]{1,0:T(8,128)S(1)} %copy.21), kind=kLoop, calls=%fused_computation | loop fusion | flops 15532032 | bytes 638976 | tf_op jit(solution)/shard_map/reduce_sum | solution.py:29
  36.2 192.0 %all-to-all-done = bf16[16,48,7424]{2,1,0:T(8,128)(2,1)} async-done(((bf16[16,48,7424]{2,1,0:T(8,128)(2,1)}), bf16[16,48,7424]{2,1,0:T(8,128)(2,1)}, u32[]{:S(2)}, u32[]{:S(2)}) %all-to-all-start) | async-done | bytes 11403296 | tf_op jit(solution)/shard_map/all_to_all | solution.py:9
  228.3 10.6 %fusion.7 = f32[128,7424]{0,1:T(8,128)} fusion(bf16[128,768]{1,0:T(8,128)(2,1)S(1)} %get-tuple-element.5, bf16[768,7424]{1,0:T(8,128)(2,1)} %bitcast), kind=kOutput, calls=%fused_computation.14 | convolution fusion | flops 1459617792 | bytes 15400960 | tf_op jit(solution)/shard_map/dot_general | solution.py:35
  238.9 5.3 %copy.23 = f32[128,116,64]{1,2,0:T(8,128)} copy(f32[128,116,64]{0,2,1:T(8,128)} %bitcast.10) | data formatting | bytes 7602176 | tf_op jit(solution)/shard_map/reshape | solution.py:15
  244.2 0.0 copy-start.2
  244.2 0.0 all-gather.2.cloned.1.call-done
  244.2 7.8 %fusion.8 = f32[128,7424]{1,0:T(8,128)} fusion(bf16[128,768]{1,0:T(8,128)(2,1)S(1)} %get-tuple-element.5, bf16[768,7424]{1,0:T(8,128)(2,1)} %all-gather.2.cloned.1.call-done), kind=kOutput, calls=%fused_computation.15 | convolution fusion | flops 1459617792 | bytes 15400960 | tf_op jit(solution)/shard_map/dot_general | solution.py:30
  252.0 0.0 all-reduce.3.cloned.1.call-update
  252.0 0.0 copy-done.2
  252.0 22.0 %all_gather.7 = bf16[768,116]{1,0:T(8,128)(2,1)S(1)} all-gather(bf16[48,116]{1,0:T(8,128)(2,1)S(1)} %copy-done.2), channel_id=1, replica_groups=mesh['geo'=8,'dist'=16] {'dist'}, dimensions={0}, use_global_device_ids=true | all-gather | bytes 189312 | tf_op jit(solution)/shard_map/all_gather | solution.py:40
  274.0 0.4 fusion.6
  274.4 27.7 %psum.23 = f32[128,116]{0,1:T(8,128)S(1)} all-reduce(f32[128,116]{0,1:T(8,128)S(1)} %fusion.6), channel_id=1, replica_groups=mesh['geo'=8,'dist'=16] {'geo'}, use_global_device_ids=true, to_apply=%region_4.0 | all-reduce | flops 14848 | bytes 118784 | tf_op jit(solution)/shard_map/psum | solution.py:43
  302.0 0.1 copy.25
  302.2 53.8 %all-reduce.3.cloned.1.call-done = (f32[128,7424]{1,0:T(8,128)}, f32[128,116,64]{1,2,0:T(8,128)}) async-done(((f32[128,7424]{1,0:T(8,128)}, f32[128,116,64]{1,2,0:T(8,128)}), (f32[128,7424]{1,0:T(8,128)}, f32[128,116,64]{1,2,0:T(8,128)})) %all-reduce.3.cloned.1.call-update) | async-done | bytes 7602192 | tf_op jit(solution)/shard_map/psum | solution.py:43
  355.9 20.0 %multiply_add_fusion = f32[128,116,116]{2,1,0:T(8,128)} fusion(f32[116,116]{1,0:T(8,128)S(1)} %fusion.4, f32[128,116]{1,0:T(8,128)S(1)} %copy.25, f32[128,116,64]{1,2,0:T(8,128)} %get-tuple-element.7), kind=kOutput, calls=%fused_computation.3 | convolution fusion | flops 1326223360 | bytes 10803776 | tf_op jit(solution)/shard_map/dik,djk->dij/dot_general | solution.py:16
  375.9 8.5 %reshape.30 = f32[128,13456]{1,0:T(8,128)} reshape(f32[128,116,116]{2,1,0:T(8,128)} %multiply_add_fusion) | data formatting | bytes 13778944 | tf_op jit(solution)/shard_map/reshape | solution.py:18
  384.5 8.2 %copy.28 = f32[128,13456]{0,1:T(8,128)} copy(f32[128,13456]{1,0:T(8,128)} %reshape.30) | data formatting | bytes 13778944 | tf_op jit(solution)/shard_map/reshape | solution.py:18
  392.7 4.2 %copy.31 = f32[128,7424]{1,0:T(8,128)} copy(f32[128,7424]{1,0:T(8,128)} %get-tuple-element.10) | data formatting | bytes 7602176
  (3 shorter events, 0.0 us)
Async XLA Ops:
  7.2 237.0 %all-gather.2.cloned.1.call-start = ((), (), s32[]{:S(2)}) async-start(), calls=%async_computation.1 | async-start | bytes 12115968 | tf_op jit(solution)/shard_map/all_gather | solution.py:32
  13.9 8.8 %copy-start = (s32[128,32]{0,1:T(8,128)S(1)}, s32[128,32]{0,1:T(8,128)}, u32[]{:S(2)}) copy-start(s32[128,32]{0,1:T(8,128)} %param.9) | copy-start | bytes 49156
  13.9 9.1 %copy-start.1 = (s32[128,32]{0,1:T(8,128)S(1)}, s32[128,32]{0,1:T(8,128)}, u32[]{:S(2)}) copy-start(s32[128,32]{0,1:T(8,128)} %param.8) | copy-start | bytes 49156
  13.9 214.4 %all-to-all-start = ((bf16[16,48,7424]{2,1,0:T(8,128)(2,1)}), bf16[16,48,7424]{2,1,0:T(8,128)(2,1)}, u32[]{:S(2)}, u32[]{:S(2)}) async-start(bf16[16,48,7424]{2,1,0:T(8,128)(2,1)} %stack.2), calls=%async_computation | async-start | bytes 22806528 | tf_op jit(solution)/shard_map/all_to_all | solution.py:9
  22.7 333.3 %all-reduce.3.cloned.1.call-start = ((), (), s32[]{:S(2)}) async-start(), calls=%async_computation.2 | async-start | bytes 15990784 | tf_op jit(solution)/shard_map/psum | solution.py:43
  244.2 7.8 %copy-start.2 = (bf16[48,116]{1,0:T(8,128)(2,1)S(1)}, bf16[48,116]{1,0:T(8,128)(2,1)}, u32[]{:S(2)}) copy-start(bf16[48,116]{1,0:T(8,128)(2,1)} %param.7) | copy-start | bytes 33412
Sparse Core Ops, SparseCore 0:
  10.1 230.5 all-gather.1
  252.1 103.7 all-reduce.2
